TPU v7x, 32 devices: a whole 2x2x4 slice. The times are simulated.
32 devices in a mesh: head: 4 (over z), blk: 8 (over y, x, core).
Axes of the slice: x: 2, y: 2, z: 4, core: 2. Of those that a mesh axis runs over, the one named last changes fastest.
Arguments:
- tokens: bfloat16 [8192, 1024], P(('blk', 'head')), may hold values from -6 to 6
- cotangent: bfloat16 [8192, 1024], P(('blk', 'head')), may hold values from -6 to 6
- segment: int32 [8192], replicated, may hold values from 0 to 3, never falling along the last dimension, each value on 1 to 6144 neighbouring positions
- norm_gain: bfloat16 [1024], P(('head', 'blk')), may hold values from 0.5 to 1.5
- norm_shift: bfloat16 [1024], P(('head', 'blk')), may hold values from -1.5 to 1.5
- in_weight: bfloat16 [1024, 3072], P(('head', 'blk')), may hold values from -0.1875 to 0.1875
- query_bias: bfloat16 [1024], P(('head', 'blk')), may hold values from -2.5 to 2.5
- value_bias: bfloat16 [1024], P(('head', 'blk')), may hold values from -1.5 to 1.5
- out_weight: bfloat16 [1024, 1024], P(('head', 'blk')), may hold values from -3 to 3
- out_bias: bfloat16 [1024], P(('head', 'blk')), may hold values from -1.5 to 1.5
- post_gain: bfloat16 [1024], P(('head', 'blk')), may hold values from 0.5 to 1.5
- post_shift: bfloat16 [1024], P(('head', 'blk')), may hold values from -1.5 to 1.5
- up_weight: bfloat16 [1024, 4096], P(('head', 'blk')), may hold values from -0.1875 to 0.1875
- up_bias: bfloat16 [4096], P(('head', 'blk')), may hold values from -1.5 to 1.5
- down_weight: bfloat16 [4096, 1024], P(('head', 'blk')), may hold values from -0.09375 to 0.09375
- down_bias: bfloat16 [1024], P(('head', 'blk')), may hold values from -1.5 to 1.5
Outputs:
- output: bfloat16 [8192, 1024], P(('blk', 'head'))
- tokens_grad: bfloat16 [8192, 1024], P(('blk', 'head'))
- norm_gain_grad: float32 [1024], P(('head', 'blk'))
- norm_shift_grad: float32 [1024], P(('head', 'blk'))
- in_weight_grad: float32 [1024, 3072], P(('head', 'blk'))
- query_bias_grad: float32 [1024], P(('head', 'blk'))
- value_bias_grad: float32 [1024], P(('head', 'blk'))
- out_weight_grad: float32 [1024, 1024], P(('head', 'blk'))
- out_bias_grad: float32 [1024], P(('head', 'blk'))
- post_gain_grad: float32 [1024], P(('head', 'blk'))
- post_shift_grad: float32 [1024], P(('head', 'blk'))
- up_weight_grad: float32 [1024, 4096], P(('head', 'blk'))
- up_bias_grad: float32 [4096], P(('head', 'blk'))
- down_weight_grad: float32 [4096, 1024], P(('head', 'blk'))
- down_bias_grad: float32 [1024], P(('head', 'blk'))
Inputs may be any that keep to these rules, and one draw needn't show every extreme that they name: `segment`: document numbers never fall along the sequence; each document holds 1 to 6144 tokens and one holds exactly 6144.
All inputs are finite; a program needn't handle non-finite values.
Results may differ from a plain program's by a relative error of at most 0.019.
Values may be sent and summed in bfloat16 or wider, within the bound.
No kernel may reach another device: no remote copies, remote signals or barrier semaphores. Data moves between devices by JAX's collectives and lax.ppermute only.
A program may use at most 256 MiB of HBM per device.

v0:
```python
import jax
import jax.numpy as jnp
from jax import lax
from jax.sharding import PartitionSpec as P

HEADS = 16
HEAD_DIM = 64
EPS = 1e-05
NEGATIVE = -1e30
GELU_C = 0.7978845608028654


def norm_forward(rows, gain, shift):
    center = rows - jnp.mean(rows, axis=-1, keepdims=True)
    var = jnp.mean(center * center, axis=-1, keepdims=True)
    inverse = lax.rsqrt(var + EPS)
    unit = center * inverse
    return (unit * gain + shift, unit, inverse)


def norm_backward(grad, unit, inverse, gain):
    scaled = grad * gain
    inner = (
        scaled
        - jnp.mean(scaled, axis=-1, keepdims=True)
        - unit * jnp.mean(scaled * unit, axis=-1, keepdims=True)
    )
    return (inverse * inner, jnp.sum(grad * unit, axis=0), jnp.sum(grad, axis=0))


def gelu_parts(pre):
    cubic = pre * pre * pre
    tangent = jnp.tanh(GELU_C * (pre + 0.044715 * cubic))
    value = 0.5 * pre * (1.0 + tangent)
    slope = 0.5 * (1.0 + tangent) + 0.5 * pre * (1.0 - tangent * tangent) * GELU_C * (
        1.0 + 3.0 * 0.044715 * pre * pre
    )
    return (value, slope)


def on_device(
    tokens,
    cotangent,
    segment,
    norm_gain,
    norm_shift,
    in_weight,
    query_bias,
    value_bias,
    out_weight,
    out_bias,
    post_gain,
    post_shift,
    up_weight,
    up_bias,
    down_weight,
    down_bias,
):
    n_head = lax.axis_size("head")
    n_blk = lax.axis_size("blk")
    group = lax.axis_index("blk")
    tok_rows = tokens.shape[0]
    width = tokens.shape[1]
    block_rows = tok_rows * n_head
    head_group = HEADS // n_head
    group_width = head_group * HEAD_DIM
    scale = HEAD_DIM ** (-0.5)
    q_first = group * block_rows
    f32 = jnp.float32
    bf16 = jnp.bfloat16
    gain_a, shift_a, w_in, bias_q, bias_v, w_out, bias_out = (
        lax.all_gather(norm_gain, ("head", "blk"), axis=0, tiled=True),
        lax.all_gather(norm_shift, ("head", "blk"), axis=0, tiled=True),
        lax.all_gather(in_weight, ("head", "blk"), axis=0, tiled=True),
        lax.all_gather(query_bias, ("head", "blk"), axis=0, tiled=True),
        lax.all_gather(value_bias, ("head", "blk"), axis=0, tiled=True),
        lax.all_gather(out_weight, ("head", "blk"), axis=0, tiled=True),
        lax.all_gather(out_bias, ("head", "blk"), axis=0, tiled=True),
    )
    rows = tokens.astype(f32)
    normed, unit_in, inverse_in = norm_forward(rows, gain_a.astype(f32), shift_a.astype(f32))
    normed_low = normed.astype(bf16)
    bias_full = jnp.concatenate([bias_q, jnp.zeros((width,), bf16), bias_v]).astype(f32)
    projected = (jnp.dot(normed_low, w_in, preferred_element_type=f32) + bias_full).astype(bf16)
    grouped = lax.all_to_all(
        projected.reshape(tok_rows, 3, n_head, group_width),
        "head",
        split_axis=2,
        concat_axis=0,
        tiled=True,
    )
    grouped = grouped.reshape(block_rows, 3, head_group, HEAD_DIM)
    queries = grouped[:, 0]
    kv_local = grouped[:, 1:].reshape(block_rows, 2, group_width)
    seg_query = lax.dynamic_slice_in_dim(segment, q_first, block_rows)
    first_doc = seg_query[0]
    query_pos = q_first + lax.iota(jnp.int32, block_rows)

    def block_scores(keys, key_start):
        key_pos = key_start + lax.iota(jnp.int32, block_rows)
        seg_key = lax.dynamic_slice_in_dim(segment, key_start, block_rows)
        allowed = (key_pos[None, :] <= query_pos[:, None]) & (
            seg_key[None, :] == seg_query[:, None]
        )
        scores = jnp.einsum("qhd,khd->hqk", queries, keys, preferred_element_type=f32) * scale
        return (scores, allowed[None])

    def visible(key_start):
        last_doc = lax.dynamic_index_in_dim(segment, key_start + block_rows - 1, keepdims=False)
        return (key_start <= q_first + block_rows - 1) & (last_doc >= first_doc)

    def split_pair(block):
        pair = block.reshape(block_rows, 2, head_group, HEAD_DIM)
        return (pair[:, 0], pair[:, 1])

    start_state = (
        jnp.zeros((block_rows, head_group, HEAD_DIM), f32),
        jnp.full((head_group, block_rows), NEGATIVE, f32),
        jnp.zeros((head_group, block_rows), f32),
    )
    piece = lax.all_gather(kv_local, "blk", axis=0, tiled=True)
    count = piece.shape[0] // block_rows
    blocks = piece.reshape(count, block_rows, 2, group_width)

    def forward_advance(state, item):
        block, index = item
        key_start = index * block_rows

        def forward_update(inner):
            acc, run_max, run_sum = inner
            keys, values = split_pair(block)
            scores, allowed = block_scores(keys, key_start)
            new_max = jnp.maximum(run_max, jnp.max(jnp.where(allowed, scores, NEGATIVE), axis=2))
            weights = jnp.where(allowed, jnp.exp(scores - new_max[:, :, None]), 0.0)
            factor = jnp.exp(run_max - new_max)
            new_sum = run_sum * factor + jnp.sum(weights, axis=2)
            mixed = jnp.einsum(
                "hqk,khd->qhd", weights.astype(bf16), values, preferred_element_type=f32
            )
            return (acc * factor.T[:, :, None] + mixed, new_max, new_sum)

        return (lax.cond(visible(key_start), forward_update, lambda inner: inner, state), None)

    state, _ = lax.scan(forward_advance, start_state, (blocks, jnp.arange(count, dtype=jnp.int32)))
    acc, run_max, run_sum = state
    attended = acc / run_sum.T[:, :, None]
    log_total = run_max + jnp.log(run_sum)
    attended_low = attended.astype(bf16)
    back_rows = lax.all_to_all(
        attended_low.reshape(block_rows, 1, group_width),
        "head",
        split_axis=0,
        concat_axis=1,
        tiled=True,
    )
    back_rows = back_rows.reshape(tok_rows, width)
    branch = jnp.dot(back_rows, w_out, preferred_element_type=f32) + bias_out.astype(f32)
    middle = rows + branch
    gain_b, shift_b, w_up, bias_up, w_down, bias_down = (
        lax.all_gather(post_gain, ("head", "blk"), axis=0, tiled=True),
        lax.all_gather(post_shift, ("head", "blk"), axis=0, tiled=True),
        lax.all_gather(up_weight, ("head", "blk"), axis=0, tiled=True),
        lax.all_gather(up_bias, ("head", "blk"), axis=0, tiled=True),
        lax.all_gather(down_weight, ("head", "blk"), axis=0, tiled=True),
        lax.all_gather(down_bias, ("head", "blk"), axis=0, tiled=True),
    )
    hidden_in, unit_mid, inverse_mid = norm_forward(middle, gain_b.astype(f32), shift_b.astype(f32))
    hidden_low = hidden_in.astype(bf16)
    pre = jnp.dot(hidden_low, w_up, preferred_element_type=f32) + bias_up.astype(f32)
    act, slope = gelu_parts(pre)
    act_low = act.astype(bf16)
    result = middle + jnp.dot(act_low, w_down, preferred_element_type=f32) + bias_down.astype(f32)
    output = result.astype(bf16)
    grad_out = cotangent.astype(f32)
    down_bias_grad = jnp.sum(grad_out, axis=0)
    down_weight_grad = jnp.einsum("tf,td->fd", act_low, cotangent, preferred_element_type=f32)
    grad_act = jnp.einsum("td,fd->tf", cotangent, w_down, preferred_element_type=f32)
    grad_pre = (grad_act * slope).astype(bf16)
    up_bias_grad = jnp.sum(grad_pre.astype(f32), axis=0)
    up_weight_grad = jnp.einsum("td,tf->df", hidden_low, grad_pre, preferred_element_type=f32)
    grad_hidden = jnp.einsum("tf,df->td", grad_pre, w_up, preferred_element_type=f32)
    grad_mid_in, post_gain_grad, post_shift_grad = norm_backward(
        grad_hidden, unit_mid, inverse_mid, gain_b.astype(f32)
    )
    grad_middle = grad_out + grad_mid_in
    (
        post_gain_grad,
        post_shift_grad,
        up_weight_grad,
        up_bias_grad,
        down_weight_grad,
        down_bias_grad,
    ) = (
        lax.psum_scatter(post_gain_grad, ("head", "blk"), scatter_dimension=0, tiled=True),
        lax.psum_scatter(post_shift_grad, ("head", "blk"), scatter_dimension=0, tiled=True),
        lax.psum_scatter(up_weight_grad, ("head", "blk"), scatter_dimension=0, tiled=True),
        lax.psum_scatter(up_bias_grad, ("head", "blk"), scatter_dimension=0, tiled=True),
        lax.psum_scatter(down_weight_grad, ("head", "blk"), scatter_dimension=0, tiled=True),
        lax.psum_scatter(down_bias_grad, ("head", "blk"), scatter_dimension=0, tiled=True),
    )
    grad_branch = grad_middle.astype(bf16)
    out_bias_grad = jnp.sum(grad_branch.astype(f32), axis=0)
    out_weight_grad = jnp.einsum("td,te->de", back_rows, grad_branch, preferred_element_type=f32)
    grad_back = jnp.einsum("te,de->td", grad_branch, w_out, preferred_element_type=f32).astype(bf16)
    grad_heads = lax.all_to_all(
        grad_back.reshape(tok_rows, n_head, group_width),
        "head",
        split_axis=1,
        concat_axis=0,
        tiled=True,
    )
    grad_heads = grad_heads.reshape(block_rows, head_group, HEAD_DIM)
    delta = jnp.sum(grad_heads.astype(f32) * attended, axis=-1).T

    def block_backward(block, key_start):
        keys, values = split_pair(block)
        scores, allowed = block_scores(keys, key_start)
        probs = jnp.where(allowed, jnp.exp(scores - log_total[:, :, None]), 0.0)
        grad_probs = jnp.einsum("qhd,khd->hqk", grad_heads, values, preferred_element_type=f32)
        grad_scores = (probs * (grad_probs - delta[:, :, None])).astype(bf16)
        grad_values = jnp.einsum(
            "hqk,qhd->khd", probs.astype(bf16), grad_heads, preferred_element_type=f32
        )
        grad_keys = (
            jnp.einsum("hqk,qhd->khd", grad_scores, queries, preferred_element_type=f32) * scale
        )
        query_add = (
            jnp.einsum("hqk,khd->qhd", grad_scores, keys, preferred_element_type=f32) * scale
        )
        return (query_add, jnp.stack([grad_keys, grad_values], axis=1))

    back_state = (
        jnp.zeros((block_rows, head_group, HEAD_DIM), f32),
        jnp.zeros((block_rows * n_blk, 2, head_group, HEAD_DIM), f32),
    )
    piece = lax.all_gather(kv_local, "blk", axis=0, tiled=True)
    count = piece.shape[0] // block_rows
    blocks = piece.reshape(count, block_rows, 2, group_width)

    def backward_advance(state, item):
        block, index = item
        key_start = index * block_rows

        def backward_update(inner):
            grad_query, grad_pairs = inner
            query_add, pair_add = block_backward(block, key_start)
            current = lax.dynamic_slice_in_dim(grad_pairs, key_start, block_rows, 0)
            return (
                grad_query + query_add,
                lax.dynamic_update_slice_in_dim(grad_pairs, current + pair_add, key_start, 0),
            )

        return (lax.cond(visible(key_start), backward_update, lambda inner: inner, state), None)

    state, _ = lax.scan(backward_advance, back_state, (blocks, jnp.arange(count, dtype=jnp.int32)))
    grad_query, grad_pairs = state
    pair_sums = lax.psum_scatter(
        grad_pairs.reshape(block_rows * n_blk, 2, group_width).astype(jnp.bfloat16),
        "blk",
        scatter_dimension=0,
        tiled=True,
    ).astype(jnp.float32)
    grad_joint = jnp.concatenate(
        [grad_query.reshape(block_rows, 1, group_width).astype(bf16), pair_sums.astype(bf16)],
        axis=1,
    )
    grad_rows = lax.all_to_all(
        grad_joint.reshape(block_rows, 3, 1, group_width),
        "head",
        split_axis=0,
        concat_axis=2,
        tiled=True,
    )
    grad_proj = grad_rows.reshape(tok_rows, 3 * width)
    query_bias_grad = jnp.sum(grad_proj[:, :width].astype(f32), axis=0)
    value_bias_grad = jnp.sum(grad_proj[:, 2 * width :].astype(f32), axis=0)
    in_weight_grad = jnp.einsum("td,te->de", normed_low, grad_proj, preferred_element_type=f32)
    grad_normed = jnp.einsum("te,de->td", grad_proj, w_in, preferred_element_type=f32)
    grad_rows_in, norm_gain_grad, norm_shift_grad = norm_backward(
        grad_normed, unit_in, inverse_in, gain_a.astype(f32)
    )
    tokens_grad = (grad_middle + grad_rows_in).astype(bf16)
    (
        norm_gain_grad,
        norm_shift_grad,
        in_weight_grad,
        query_bias_grad,
        value_bias_grad,
        out_weight_grad,
        out_bias_grad,
    ) = (
        lax.psum_scatter(norm_gain_grad, ("head", "blk"), scatter_dimension=0, tiled=True),
        lax.psum_scatter(norm_shift_grad, ("head", "blk"), scatter_dimension=0, tiled=True),
        lax.psum_scatter(in_weight_grad, ("head", "blk"), scatter_dimension=0, tiled=True),
        lax.psum_scatter(query_bias_grad, ("head", "blk"), scatter_dimension=0, tiled=True),
        lax.psum_scatter(value_bias_grad, ("head", "blk"), scatter_dimension=0, tiled=True),
        lax.psum_scatter(out_weight_grad, ("head", "blk"), scatter_dimension=0, tiled=True),
        lax.psum_scatter(out_bias_grad, ("head", "blk"), scatter_dimension=0, tiled=True),
    )
    return (
        output,
        tokens_grad,
        norm_gain_grad,
        norm_shift_grad,
        in_weight_grad,
        query_bias_grad,
        value_bias_grad,
        out_weight_grad,
        out_bias_grad,
        post_gain_grad,
        post_shift_grad,
        up_weight_grad,
        up_bias_grad,
        down_weight_grad,
        down_bias_grad,
    )


def solution(mesh):
    placed = (
        P(("blk", "head"), None),
        P(("blk", "head"), None),
        P(),
        P(("head", "blk")),
        P(("head", "blk")),
        P(("head", "blk"), None),
        P(("head", "blk")),
        P(("head", "blk")),
        P(("head", "blk"), None),
        P(("head", "blk")),
        P(("head", "blk")),
        P(("head", "blk")),
        P(("head", "blk"), None),
        P(("head", "blk")),
        P(("head", "blk"), None),
        P(("head", "blk")),
    )
    return jax.shard_map(
        on_device,
        mesh=mesh,
        in_specs=placed,
        out_specs=(
            P(("blk", "head"), None),
            P(("blk", "head"), None),
            P(("head", "blk")),
            P(("head", "blk")),
            P(("head", "blk"), None),
            P(("head", "blk")),
            P(("head", "blk")),
            P(("head", "blk"), None),
            P(("head", "blk")),
            P(("head", "blk")),
            P(("head", "blk")),
            P(("head", "blk"), None),
            P(("head", "blk")),
            P(("head", "blk"), None),
            P(("head", "blk")),
        ),
        check_vma=False,
    )
```

profile of v0, /device:TPU:14, one launch (start us, length us, event | category | flops | bytes accessed | tf_op | source)
XLA Modules:
  0.0 1566.0 jit_solution(17215553345524749497)
XLA Ops:
  14.7 41.5 %all-reduce.18 = (bf16[1024]{0:T(1024)(128)(2,1)S(1)}, bf16[1024]{0:T(1024)(128)(2,1)S(1)}, bf16[1024]{0:T(1024)(128)(2,1)S(1)}, bf16[1024]{0:T(1024)(128)(2,1)S...) all-reduce(bf16[1024]{0:T(1024)(128)(2,1)S(1)} %dynamic-update-slic, ...), channel_id=1, replica_groups=mesh['head'=4,'blk'=8] {'head','blk'}, use_global_device_ids=true, to_apply=%add.3 | all-reduce | flops 8192 | bytes 32768
  59.0 21.8 %all-gather.7.cloned.1.call-done = bf16[1024,3072]{1,0:T(8,128)(2,1)} async-done(((bf16[32,3072]{1,0:T(8,128)(2,1)}), bf16[1024,3072]{1,0:T(8,128)(2,1)}) %all-gather.7.cloned.1.call-update) | async-done | bytes 6291472 | tf_op jit(solution)/shard_map/all_gather | solution.py:74
  80.7 6.0 fusion.44
  86.8 3.2 reshape.282
  90.3 39.0 %all_to_all.60 = bf16[256,3,4,256]{3,0,1,2:T(8,128)(2,1)S(1)} all-to-all(bf16[256,3,4,256]{3,0,1,2:T(8,128)(2,1)S(1)} %copy.93), channel_id=1, replica_groups=mesh['head'=4,'blk'=8] {'head'}, dimensions={2} | all-to-all | bytes 3145728 | tf_op jit(solution)/shard_map/all_to_all | solution.py:85
  131.5 2.8 reshape.283
  138.6 50.8 %all-gather.9.cloned.1.call-done = bf16[8192,2,256]{0,2,1:T(8,128)(2,1)} async-done(((bf16[1024,2,256]{0,2,1:T(8,128)(2,1)}), bf16[8192,2,256]{0,2,1:T(8,128)(2,1)}) %all-gather.9.cloned.1.call-update) | async-done | bytes 8388624 | tf_op jit(solution)/shard_map/all_gather | solution.py:121
  189.4 12.0 copy.95
  201.4 11.5 copy.96
  213.1 45.0 %while.38 = (s32[]{:T(128)}, f32[1024,4,64]{0,2,1:T(8,128)S(1)}, f32[4,1024]{1,0:T(4,128)S(1)}, f32[4,1024]{1,0:T(4,128)S(1)}, s32[8]{0:T(128)S(1)}, /*index=5*/...) while((s32[]{:T(128)}, f32[1024,4,64]{0,2,1:T(8,128)S(1)}, ...), condition=%wide.region_7.8_spmd.clone, body=%wide.region_2.7_spmd.clone.sunk | while | flops 1123563520 | bytes 60596688 | solution.py:144
  240.2 13.9 conditional.6
  243.5 3.0 fusion.4
  246.5 3.9 fusion.15
  250.4 3.7 fusion.7
  260.9 5.1 all-to-all-start.1
  266.1 95.4 %all-gather = bf16[32,1,128]{2,1,0:T(2,128)(2,1)S(1)} all-gather(bf16[1,1,128]{2,1,0:T(2,128)(2,1)S(1)} %bitcast.161), channel_id=1, replica_groups=mesh['head'=4,'blk'=8] {'head','blk'}, dimensions={0}, use_global_device_ids=true | all-gather | bytes 8448 | tf_op jit(solution)/shard_map/all_gather | solution.py:163
  366.6 2.8 fusion.71
  369.8 8.0 convolution_add_fusion
  377.8 39.5 %all-gather.15.cloned.1.call-done = bf16[4096,1024]{1,0:T(8,128)(2,1)} async-done(((bf16[128,1024]{1,0:T(8,128)(2,1)}), bf16[4096,1024]{1,0:T(8,128)(2,1)}) %all-gather.15.cloned.1.call-update) | async-done | bytes 8388624 | tf_op jit(solution)/shard_map/all_gather | solution.py:164
  417.3 11.8 convert_reduce_fusion
  429.2 3.2 multiply_reduce_fusion
  436.1 4.0 all-to-all-start.2
  440.0 12.0 all-to-all-done.2
  455.9 7.8 broadcast_in_dim.56
  463.7 81.5 %while.39 = (s32[]{:T(128)}, f32[1024,4,64]{0,2,1:T(8,128)}, f32[8192,2,4,64]{0,3,2,1:T(8,128)}, s32[8]{0:T(128)S(1)}, s32[]{:T(128)}, /*index=5*/s32[8192]{0:T(...) while((s32[]{:T(128)}, f32[1024,4,64]{0,2,1:T(8,128)}, ...), condition=%wide.region_16.17_spmd.clone, body=%wide.region_13.16_spmd.clone.sunk | while | flops 2731280384 | bytes 103375360 | solution.py:255
  490.9 50.1 %conditional.7 = ((f32[1024,4,64]{0,2,1:T(8,128)}, f32[8192,2,4,64]{0,3,2,1:T(8,128)})) conditional(s32[]{:T(128)} %convert_element_type.245, (f32[1024,4,64]{0,2,1:T(8,128)}, f32[8192,2,4,64]{0,3,2,1:T(8,128)}) %tuple.143, (s32[]{:T(128)}, s32[]{:T(128)}, s32[8192]{0:T(1024)}, s32[1024]{0:T(1024)S(1)}, bf16[8,1024,2,256]{1,3,2,0:T(8,128)(2,1)}, ...), branch_computations={%region_14.14_spmd, %region_15.15_spmd} | conditional | flops 2731280384 | bytes 103370856 | solution.py:253
  494.2 8.1 fusion.33
  502.3 10.3 fusion.27
  512.6 9.1 fusion.22
  521.7 3.9 fusion.31
  525.6 2.7 fusion.32
  530.6 10.4 dynamic_update_slice.3
  545.1 9.0 convert_element_type.157
  555.4 2.7 fusion.63
  559.5 316.2 %reduce-scatter.6.cloned.1.call-done = bf16[1024,2,256]{0,2,1:T(8,128)(2,1)} async-done(((bf16[8192,2,256]{0,2,1:T(8,128)(2,1)}), bf16[1024,2,256]{0,2,1:T(8,128)(2,1)}) %reduce-scatter.6.cloned.1.call-update) | async-done | bytes 1048592 | tf_op jit(solution)/shard_map/reduce_scatter | solution.py:257
  875.7 2.5 maximum_bitcast_fusion
  878.2 4.1 copy.102
  882.3 59.2 %all_to_all.61 = bf16[1024,3,1,256]{3,1,2,0:T(4,128)(2,1)S(1)} all-to-all(bf16[1024,3,1,256]{3,1,2,0:T(4,128)(2,1)} %copy.102), channel_id=1, replica_groups=mesh['head'=4,'blk'=8] {'head'}, dimensions={0} | all-to-all | bytes 3145728 | tf_op jit(solution)/shard_map/all_to_all | solution.py:267
  943.0 2.6 copy.104
  945.6 7.9 fusion.66
  954.6 10.8 fusion.70
  966.6 9.8 fusion.69
  977.1 8.4 fusion.46
  985.9 5.1 fusion.60
  991.0 41.1 %all-reduce.17 = (f32[1024]{0:T(1024)S(1)}, f32[1024]{0:T(1024)S(1)}, f32[1024]{0:T(1024)S(1)}, f32[1024]{0:T(1024)S(1)}, f32[1024]{0:T(1024)S(1)}, /*index=5*/f...) all-reduce(f32[1024]{0:T(1024)S(1)} %get-tuple-element.973, ...), channel_id=3, replica_groups=mesh['head'=4,'blk'=8] {'head','blk'}, use_global_device_ids=true, to_apply=%region_21.22.clone | all-reduce | flops 12288 | bytes 98304
  1038.5 145.6 %reduce-scatter.8.cloned.1.call-done = f32[32,3072]{1,0:T(8,128)} async-done(((f32[1024,3072]{1,0:T(8,128)}), f32[32,3072]{1,0:T(8,128)}) %reduce-scatter.8.cloned.1.call-update) | async-done | bytes 393232 | tf_op jit(solution)/shard_map/reduce_scatter | solution.py:294
  1184.1 187.4 %reduce-scatter.14.cloned.1.call-done = f32[128,1024]{1,0:T(8,128)} async-done(((f32[4096,1024]{1,0:T(8,128)}), f32[128,1024]{1,0:T(8,128)}) %reduce-scatter.14.cloned.1.call-update) | async-done | bytes 524304 | tf_op jit(solution)/shard_map/reduce_scatter | solution.py:198
  1371.5 187.2 %reduce-scatter.12.cloned.1.call-done = f32[32,4096]{1,0:T(8,128)} async-done(((f32[1024,4096]{1,0:T(8,128)}), f32[32,4096]{1,0:T(8,128)}) %reduce-scatter.12.cloned.1.call-update) | async-done | bytes 524304 | tf_op jit(solution)/shard_map/reduce_scatter | solution.py:196
  (247 shorter events, 85.5 us)
Async XLA Ops:
  7.2 73.5 %all-gather.7.cloned.1.call-start = ((), (), s32[]{:S(2)}) async-start(), calls=%async_computation.9 | async-start | bytes 6488064 | tf_op jit(solution)/shard_map/all_gather | solution.py:74
  7.9 181.5 %all-gather.9.cloned.1.call-start = ((), (), s32[]{:S(2)}) async-start(), calls=%async_computation.10 | async-start | bytes 9437184 | tf_op jit(solution)/shard_map/all_gather | solution.py:121
  56.2 30.6 %copy-start.17 = (f32[1024]{0:T(1024)}, f32[1024]{0:T(1024)S(1)}, u32[]{:S(2)}) copy-start(f32[1024]{0:T(1024)S(1)} %convert_element_type.136) | copy-start | bytes 12292
  56.2 30.5 %copy-start.19 = (f32[1024]{0:T(1024)}, f32[1024]{0:T(1024)S(1)}, u32[]{:S(2)}) copy-start(f32[1024]{0:T(1024)S(1)} %convert_element_type.137) | copy-start | bytes 12292
  57.4 29.3 %copy-start.23 = (f32[256]{0:T(256)}, f32[256]{0:T(256)S(1)}, u32[]{:S(2)}) copy-start(f32[256]{0:T(256)S(1)} %broadcast_multiply_fusion.5) | copy-start | bytes 3076
  58.9 27.8 %copy-start.27 = (f32[256]{0:T(256)}, f32[256]{0:T(256)S(1)}, u32[]{:S(2)}) copy-start(f32[256]{0:T(256)S(1)} %add_rsqrt_fusion.1) | copy-start | bytes 3076
  135.4 231.2 %all-gather.11.cloned.1.call-start = ((), (), s32[]{:S(2)}) async-start(), calls=%async_computation.11 | async-start | bytes 2162688 | tf_op jit(solution)/shard_map/all_gather | solution.py:77
  136.2 233.6 %all-gather.13.cloned.1.call-start = ((), (), s32[]{:S(2)}) async-start(), calls=%async_computation.12 | async-start | bytes 8650752 | tf_op jit(solution)/shard_map/all_gather | solution.py:162
  136.7 280.6 %all-gather.15.cloned.1.call-start = ((), (), s32[]{:S(2)}) async-start(), calls=%async_computation.13 | async-start | bytes 8650752 | tf_op jit(solution)/shard_map/all_gather | solution.py:164
  258.0 8.0 copy-start.35
  258.7 108.0 %copy-start.5 = (bf16[256,1024]{1,0:T(8,128)(2,1)S(1)}, bf16[256,1024]{1,0:T(8,128)(2,1)}, u32[]{:S(2)}) copy-start(bf16[256,1024]{1,0:T(8,128)(2,1)} %param.24) | copy-start | bytes 1572868
  260.9 100.6 %all-to-all-start.1 = ((bf16[4,2,32768]{2,1,0:T(2,128)(2,1)}), bf16[4,2,32768]{2,1,0:T(2,128)(2,1)}, u32[]{:S(2)}, u32[]{:S(2)}) async-start(bf16[4,2,32768]{2,1,0:T(2,128)(2,1)} %reshape.311), calls=%async_computation.1 | async-start | bytes 1048576 | tf_op jit(solution)/shard_map/all_to_all | solution.py:149
  266.0 166.3 %copy-start.13 = (f32[1024]{0:T(1024)}, f32[1024]{0:T(1024)S(1)}, u32[]{:S(2)}) copy-start(f32[1024]{0:T(1024)S(1)} %convert_element_type.143) | copy-start | bytes 12292
  266.1 103.7 %copy-start.15 = (f32[1024]{0:T(1024)}, f32[1024]{0:T(1024)S(1)}, u32[]{:S(2)}) copy-start(f32[1024]{0:T(1024)S(1)} %convert_element_type.144) | copy-start | bytes 12292
  369.5 62.9 %copy-start.1 = (f32[256,1024]{1,0:T(8,128)}, f32[256,1024]{1,0:T(8,128)S(1)}, u32[]{:S(2)}) copy-start(f32[256,1024]{1,0:T(8,128)S(1)} %get-tuple-element.1062) | copy-start | bytes 3145732
  369.5 62.9 %copy-start.21 = (f32[256]{0:T(256)}, f32[256]{0:T(256)S(1)}, u32[]{:S(2)}) copy-start(f32[256]{0:T(256)S(1)} %broadcast_multiply_fusion.4) | copy-start | bytes 3076
  369.8 62.6 %copy-start.25 = (f32[256]{0:T(256)}, f32[256]{0:T(256)S(1)}, u32[]{:S(2)}) copy-start(f32[256]{0:T(256)S(1)} %add_rsqrt_fusion) | copy-start | bytes 3076
  369.8 47.5 %copy-start.10 = (bf16[256,1024]{1,0:T(8,128)(2,1)S(1)}, bf16[256,1024]{1,0:T(8,128)(2,1)}, u32[]{:S(2)}) copy-start(bf16[256,1024]{1,0:T(8,128)(2,1)} %param.25) | copy-start | bytes 1572868
  417.3 11.8 copy-start.36
  429.2 3.2 copy-start.12
  429.2 5.3 copy-start.8
  433.5 1.0 copy-start.3
  436.1 15.9 %all-to-all-start.2 = ((bf16[256,4,256]{2,0,1:T(8,128)(2,1)}), bf16[256,4,256]{2,0,1:T(8,128)(2,1)S(1)}, u32[]{:S(2)}, u32[]{:S(2)}) async-start(bf16[256,4,256]{2,0,1:T(8,128)(2,1)} %bitcast.128), calls=%async_computation.2 | async-start | bytes 1048576 | tf_op jit(solution)/shard_map/all_to_all | solution.py:205
  440.0 435.7 %reduce-scatter.6.cloned.1.call-start = ((), (), s32[]{:S(2)}) async-start(), calls=%async_computation.14 | async-start | bytes 9437184 | tf_op jit(solution)/shard_map/reduce_scatter | solution.py:257
  525.6 2.7 copy-start
  554.1 1.2 copy-start.4
  554.1 1.4 copy-start.9
  554.1 484.4 %reduce-scatter.10.cloned.1.call-start = ((), (), s32[]{:S(2)}) async-start(), calls=%async_computation.16 | async-start | bytes 4325376 | tf_op jit(solution)/shard_map/reduce_scatter | solution.py:297
  558.1 626.0 %reduce-scatter.8.cloned.1.call-start = ((), (), s32[]{:S(2)}) async-start(), calls=%async_computation.15 | async-start | bytes 12976128 | tf_op jit(solution)/shard_map/reduce_scatter | solution.py:294
  941.6 4.0 copy-start.6
  941.6 4.0 copy-start.18
  941.6 4.0 copy-start.20
  941.6 4.0 copy-start.24
  941.6 4.0 copy-start.28
  953.5 1.0 copy-start.11
  953.5 418.0 %reduce-scatter.14.cloned.1.call-start = ((), (), s32[]{:S(2)}) async-start(), calls=%async_computation.18 | async-start | bytes 17301504 | tf_op jit(solution)/shard_map/reduce_scatter | solution.py:198
  965.3 1.2 copy-start.2
  965.3 1.2 copy-start.14
  965.3 1.2 copy-start.16
  965.3 1.2 copy-start.22
  965.4 1.2 copy-start.26
  965.4 593.3 %reduce-scatter.12.cloned.1.call-start = ((), (), s32[]{:S(2)}) async-start(), calls=%async_computation.17 | async-start | bytes 17301504 | tf_op jit(solution)/shard_map/reduce_scatter | solution.py:196
  977.1 8.4 copy-start.7
  985.8 5.1 copy-start.29
  985.8 5.1 copy-start.30
  985.8 5.1 copy-start.31
  985.8 5.1 copy-start.32
  985.8 5.1 copy-start.33
  (1 other events, 0.7 us)
Sparse Core Ops, SparseCore 0:
  10.9 69.8 all-gather.6
  135.5 53.8 all-gather.8
  192.3 55.7 all-gather.10
  250.8 83.0 all-gather.12
  336.6 80.6 all-gather.14
  554.2 321.3 reduce-scatter.5
  878.6 125.1 reduce-scatter.9
  1011.4 172.6 reduce-scatter.7
  1187.0 184.4 reduce-scatter.13
  1374.2 184.4 reduce-scatter.11
where the time goes:
time: 1580 us; the launch traced here: 1570 us
  waiting for transfers between devices  963 us (61%)
  blocking collectives  276 us (17%)
  local copies, waits for them, and re-layouts  122 us (8%)
  matrix products  118 us (7%)
  loops' own time  32.7 us (2%)
  other arithmetic  29.2 us (2%)
    reduce_scatter x1, waiting for transfers between devices, on_device(): lax.psum_scatter(grad_pairs.reshape(block_rows * n_blk, 2, group_width).a...  316 us
    reduce_scatter x1, waiting for transfers between devices, on_device(): lax.psum_scatter(down_weight_grad, ('head', 'blk'), scatter_dimension=0,...  187 us
    reduce_scatter x1, waiting for transfers between devices, on_device(): lax.psum_scatter(up_weight_grad, ('head', 'blk'), scatter_dimension=0, ti...  187 us
    reduce_scatter x1, waiting for transfers between devices, on_device(): lax.psum_scatter(in_weight_grad, ('head', 'blk'), scatter_dimension=0, ti...  146 us
    all_gather x1, blocking collectives, on_device(): lax.all_gather(up_bias, ('head', 'blk'), axis=0, tiled=True)  95.4 us
    unnamed x2, blocking collectives  82.6 us
    all_to_all x1, blocking collectives, on_device(): lax.all_to_all(grad_joint.reshape(block_rows, 3, 1, group_width), 'head',...  59.2 us
    all_gather x1, waiting for transfers between devices, on_device(): piece = lax.all_gather(kv_local, 'blk', axis=0, tiled=True)  50.8 us
  transfers between devices with their start and end apart: 12, of which 8 were waited for; matrix products, arithmetic and copies ran while one was open for 9% of the time, Pallas kernels for 0%

commit v1 on v0

--- a/solution.py
+++ b/solution.py
@@ -264,12 +264,18 @@
         [grad_query.reshape(block_rows, 1, group_width).astype(bf16), pair_sums.astype(bf16)],
         axis=1,
     )
-    grad_rows = lax.all_to_all(
-        grad_joint.reshape(block_rows, 3, 1, group_width),
-        "head",
-        split_axis=0,
-        concat_axis=2,
-        tiled=True,
+    grad_rows = jnp.concatenate(
+        lax.all_to_all(
+            jnp.stack(
+                jnp.split(
+                    grad_joint.reshape(block_rows, 3, 1, group_width), lax.axis_size("head"), axis=0
+                )
+            ),
+            "head",
+            0,
+            0,
+        ),
+        axis=2,
     )
     grad_proj = grad_rows.reshape(tok_rows, 3 * width)
     query_bias_grad = jnp.sum(grad_proj[:, :width].astype(f32), axis=0)

time: 1580 us -> 1580 us (level)
  waiting for transfers between devices: 963 us -> 984 us
    reduce_scatter x1, waiting for transfers between devices: 146 us -> 167 us  [on_device(): lax.psum_scatter(in_weight_grad, ('head', 'blk'), scatter_dimension=0, ti...]
    unnamed x103 -> x105, local copies, waits for them, and re-layouts: 32.6 us -> 34 us
where the time goes in v1:
time: 1580 us; the launch traced here: 1560 us
  waiting for transfers between devices  984 us (62%)
  blocking collectives  262 us (17%)
  matrix products  117 us (7%)
  local copies, waits for them, and re-layouts  115 us (7%)
  loops' own time  32.9 us (2%)
  other arithmetic  28.2 us (2%)
    reduce_scatter x1, waiting for transfers between devices, on_device(): lax.psum_scatter(grad_pairs.reshape(block_rows * n_blk, 2, group_width).a...  316 us
    reduce_scatter x1, waiting for transfers between devices, on_device(): lax.psum_scatter(down_weight_grad, ('head', 'blk'), scatter_dimension=0,...  187 us
    reduce_scatter x1, waiting for transfers between devices, on_device(): lax.psum_scatter(up_weight_grad, ('head', 'blk'), scatter_dimension=0, ti...  187 us
    reduce_scatter x1, waiting for transfers between devices, on_device(): lax.psum_scatter(in_weight_grad, ('head', 'blk'), scatter_dimension=0, ti...  167 us
    all_gather x1, blocking collectives, on_device(): lax.all_gather(up_bias, ('head', 'blk'), axis=0, tiled=True)  95.2 us
    unnamed x2, blocking collectives  82.5 us
    all_gather x1, waiting for transfers between devices, on_device(): piece = lax.all_gather(kv_local, 'blk', axis=0, tiled=True)  50.8 us
    all_to_all x1, blocking collectives, on_device(): lax.all_to_all(jnp.stack(jnp.split(grad_joint.reshape(block_rows, 3, 1, g...  45.7 us
  transfers between devices with their start and end apart: 12, of which 8 were waited for; matrix products, arithmetic and copies ran while one was open for 9% of the time, Pallas kernels for 0%

profile of v1, /device:TPU:14, one launch (start us, length us, event | category | flops | bytes accessed | tf_op | source)
XLA Modules:
  0.0 1564.3 jit_solution(10832903660457688252)
XLA Ops:
  14.7 41.5 %all-reduce.18 = (bf16[1024]{0:T(1024)(128)(2,1)S(1)}, bf16[1024]{0:T(1024)(128)(2,1)S(1)}, bf16[1024]{0:T(1024)(128)(2,1)S(1)}, bf16[1024]{0:T(1024)(128)(2,1)S...) all-reduce(bf16[1024]{0:T(1024)(128)(2,1)S(1)} %dynamic-update-slic, ...), channel_id=1, replica_groups=mesh['head'=4,'blk'=8] {'head','blk'}, use_global_device_ids=true, to_apply=%add.3 | all-reduce | flops 8192 | bytes 32768
  59.0 21.8 %all-gather.7.cloned.1.call-done = bf16[1024,3072]{1,0:T(8,128)(2,1)} async-done(((bf16[32,3072]{1,0:T(8,128)(2,1)}), bf16[1024,3072]{1,0:T(8,128)(2,1)}) %all-gather.7.cloned.1.call-update) | async-done | bytes 6291472 | tf_op jit(solution)/shard_map/all_gather | solution.py:74
  80.7 6.0 fusion.44
  86.8 3.2 reshape.287
  90.3 39.0 %all_to_all.50 = bf16[256,3,4,256]{3,0,1,2:T(8,128)(2,1)S(1)} all-to-all(bf16[256,3,4,256]{3,0,1,2:T(8,128)(2,1)S(1)} %copy.95), channel_id=1, replica_groups=mesh['head'=4,'blk'=8] {'head'}, dimensions={2} | all-to-all | bytes 3145728 | tf_op jit(solution)/shard_map/all_to_all | solution.py:85
  129.3 2.2 copy.96
  131.5 2.8 reshape.288
  138.6 50.8 %all-gather.9.cloned.1.call-done = bf16[8192,2,256]{0,2,1:T(8,128)(2,1)} async-done(((bf16[1024,2,256]{0,2,1:T(8,128)(2,1)}), bf16[8192,2,256]{0,2,1:T(8,128)(2,1)}) %all-gather.9.cloned.1.call-update) | async-done | bytes 8388624 | tf_op jit(solution)/shard_map/all_gather | solution.py:121
  189.4 12.0 copy.97
  201.4 11.5 copy.98
  213.1 45.0 %while.38 = (s32[]{:T(128)}, f32[1024,4,64]{0,2,1:T(8,128)S(1)}, f32[4,1024]{1,0:T(4,128)S(1)}, f32[4,1024]{1,0:T(4,128)S(1)}, s32[8]{0:T(128)S(1)}, /*index=5*/...) while((s32[]{:T(128)}, f32[1024,4,64]{0,2,1:T(8,128)S(1)}, ...), condition=%wide.region_7.8_spmd.clone, body=%wide.region_2.7_spmd.clone.sunk | while | flops 1123563520 | bytes 60596688 | solution.py:144
  240.2 13.9 conditional.6
  243.5 3.0 fusion.4
  246.5 3.9 fusion.15
  250.4 3.7 fusion.7
  260.9 5.1 all-to-all-start.1
  266.1 95.2 %all-gather = bf16[32,1,128]{2,1,0:T(2,128)(2,1)S(1)} all-gather(bf16[1,1,128]{2,1,0:T(2,128)(2,1)S(1)} %bitcast.165), channel_id=1, replica_groups=mesh['head'=4,'blk'=8] {'head','blk'}, dimensions={0}, use_global_device_ids=true | all-gather | bytes 8448 | tf_op jit(solution)/shard_map/all_gather | solution.py:163
  361.3 2.2 reshape.316
  366.4 2.8 fusion.78
  369.6 8.0 convolution_add_fusion
  377.6 39.7 %all-gather.15.cloned.1.call-done = bf16[4096,1024]{1,0:T(8,128)(2,1)} async-done(((bf16[128,1024]{1,0:T(8,128)(2,1)}), bf16[4096,1024]{1,0:T(8,128)(2,1)}) %all-gather.15.cloned.1.call-update) | async-done | bytes 8388624 | tf_op jit(solution)/shard_map/all_gather | solution.py:164
  417.3 11.8 convert_reduce_fusion
  429.2 3.2 multiply_reduce_fusion
  436.0 4.0 all-to-all-start.2
  440.0 12.0 all-to-all-done.2
  455.8 7.8 broadcast_in_dim.56
  463.6 81.6 %while.39 = (s32[]{:T(128)}, f32[1024,4,64]{0,2,1:T(8,128)}, f32[8192,2,4,64]{0,3,2,1:T(8,128)}, s32[8]{0:T(128)S(1)}, s32[]{:T(128)}, /*index=5*/s32[8192]{0:T(...) while((s32[]{:T(128)}, f32[1024,4,64]{0,2,1:T(8,128)}, ...), condition=%wide.region_16.17_spmd.clone, body=%wide.region_13.16_spmd.clone.sunk | while | flops 2731280384 | bytes 103375360 | solution.py:255
  491.2 50.0 %conditional.7 = ((f32[1024,4,64]{0,2,1:T(8,128)}, f32[8192,2,4,64]{0,3,2,1:T(8,128)})) conditional(s32[]{:T(128)} %convert_element_type.245, (f32[1024,4,64]{0,2,1:T(8,128)}, f32[8192,2,4,64]{0,3,2,1:T(8,128)}) %tuple.146, (s32[]{:T(128)}, s32[]{:T(128)}, s32[8192]{0:T(1024)}, s32[1024]{0:T(1024)S(1)}, bf16[8,1024,2,256]{1,3,2,0:T(8,128)(2,1)}, ...), branch_computations={%region_14.14_spmd, %region_15.15_spmd} | conditional | flops 2731280384 | bytes 103370856 | solution.py:253
  494.5 8.1 fusion.33
  502.6 10.3 fusion.27
  512.9 9.1 fusion.22
  522.0 3.9 fusion.31
  525.9 2.7 fusion.32
  528.6 2.3 maximum_add_fusion
  530.9 10.3 dynamic_update_slice.3
  545.3 9.0 convert_element_type.157
  555.6 2.7 fusion.70
  559.6 316.4 %reduce-scatter.6.cloned.1.call-done = bf16[1024,2,256]{0,2,1:T(8,128)(2,1)} async-done(((bf16[8192,2,256]{0,2,1:T(8,128)(2,1)}), bf16[1024,2,256]{0,2,1:T(8,128)(2,1)}) %reduce-scatter.6.cloned.1.call-update) | async-done | bytes 1048592 | tf_op jit(solution)/shard_map/reduce_scatter | solution.py:257
  877.6 45.7 %all_to_all.51 = bf16[4,256,3,1,256]{1,4,2,3,0:T(8,128)(2,1)S(1)} all-to-all(bf16[4,256,3,1,256]{1,4,2,3,0:T(8,128)(2,1)S(1)} %pad_maximum_fusion), channel_id=1, replica_groups=mesh['head'=4,'blk'=8] {'head'}, dimensions={0} | all-to-all | bytes 3145728 | tf_op jit(solution)/shard_map/all_to_all | solution.py:268
  924.6 6.5 fusion.73
  932.1 10.8 fusion.77
  944.2 9.8 fusion.76
  954.7 8.3 fusion.46
  963.4 5.1 fusion.60
  968.5 41.0 %all-reduce.17 = (f32[1024]{0:T(1024)S(1)}, f32[1024]{0:T(1024)S(1)}, f32[1024]{0:T(1024)S(1)}, f32[1024]{0:T(1024)S(1)}, f32[1024]{0:T(1024)S(1)}, /*index=5*/f...) all-reduce(f32[1024]{0:T(1024)S(1)} %get-tuple-element.973, ...), channel_id=3, replica_groups=mesh['head'=4,'blk'=8] {'head','blk'}, use_global_device_ids=true, to_apply=%region_21.22.clone | all-reduce | flops 12288 | bytes 98304
  1016.0 166.6 %reduce-scatter.8.cloned.1.call-done = f32[32,3072]{1,0:T(8,128)} async-done(((f32[1024,3072]{1,0:T(8,128)}), f32[32,3072]{1,0:T(8,128)}) %reduce-scatter.8.cloned.1.call-update) | async-done | bytes 393232 | tf_op jit(solution)/shard_map/reduce_scatter | solution.py:300
  1182.6 187.4 %reduce-scatter.14.cloned.1.call-done = f32[128,1024]{1,0:T(8,128)} async-done(((f32[4096,1024]{1,0:T(8,128)}), f32[128,1024]{1,0:T(8,128)}) %reduce-scatter.14.cloned.1.call-update) | async-done | bytes 524304 | tf_op jit(solution)/shard_map/reduce_scatter | solution.py:198
  1370.0 187.2 %reduce-scatter.12.cloned.1.call-done = f32[32,4096]{1,0:T(8,128)} async-done(((f32[1024,4096]{1,0:T(8,128)}), f32[32,4096]{1,0:T(8,128)}) %reduce-scatter.12.cloned.1.call-update) | async-done | bytes 524304 | tf_op jit(solution)/shard_map/reduce_scatter | solution.py:196
  (248 shorter events, 80.1 us)
Async XLA Ops:
  7.2 73.5 %all-gather.7.cloned.1.call-start = ((), (), s32[]{:S(2)}) async-start(), calls=%async_computation.9 | async-start | bytes 6488064 | tf_op jit(solution)/shard_map/all_gather | solution.py:74
  7.9 181.5 %all-gather.9.cloned.1.call-start = ((), (), s32[]{:S(2)}) async-start(), calls=%async_computation.10 | async-start | bytes 9437184 | tf_op jit(solution)/shard_map/all_gather | solution.py:121
  56.2 30.6 %copy-start.18 = (f32[1024]{0:T(1024)}, f32[1024]{0:T(1024)S(1)}, u32[]{:S(2)}) copy-start(f32[1024]{0:T(1024)S(1)} %convert_element_type.136) | copy-start | bytes 12292
  56.2 30.6 %copy-start.20 = (f32[1024]{0:T(1024)}, f32[1024]{0:T(1024)S(1)}, u32[]{:S(2)}) copy-start(f32[1024]{0:T(1024)S(1)} %convert_element_type.137) | copy-start | bytes 12292
  57.4 29.3 %copy-start.24 = (f32[256]{0:T(256)}, f32[256]{0:T(256)S(1)}, u32[]{:S(2)}) copy-start(f32[256]{0:T(256)S(1)} %broadcast_multiply_fusion.5) | copy-start | bytes 3076
  58.9 27.8 %copy-start.28 = (f32[256]{0:T(256)}, f32[256]{0:T(256)S(1)}, u32[]{:S(2)}) copy-start(f32[256]{0:T(256)S(1)} %add_rsqrt_fusion.1) | copy-start | bytes 3076
  135.4 231.0 %all-gather.11.cloned.1.call-start = ((), (), s32[]{:S(2)}) async-start(), calls=%async_computation.11 | async-start | bytes 2162688 | tf_op jit(solution)/shard_map/all_gather | solution.py:77
  136.2 233.4 %all-gather.13.cloned.1.call-start = ((), (), s32[]{:S(2)}) async-start(), calls=%async_computation.12 | async-start | bytes 8650752 | tf_op jit(solution)/shard_map/all_gather | solution.py:162
  136.8 280.6 %all-gather.15.cloned.1.call-start = ((), (), s32[]{:S(2)}) async-start(), calls=%async_computation.13 | async-start | bytes 8650752 | tf_op jit(solution)/shard_map/all_gather | solution.py:164
  258.0 8.0 copy-start.36
  258.7 107.8 %copy-start.5 = (bf16[256,1024]{1,0:T(8,128)(2,1)S(1)}, bf16[256,1024]{1,0:T(8,128)(2,1)}, u32[]{:S(2)}) copy-start(bf16[256,1024]{1,0:T(8,128)(2,1)} %param.24) | copy-start | bytes 1572868
  260.9 100.4 %all-to-all-start.1 = ((bf16[4,2,32768]{2,1,0:T(2,128)(2,1)}), bf16[4,2,32768]{2,1,0:T(2,128)(2,1)}, u32[]{:S(2)}, u32[]{:S(2)}) async-start(bf16[4,2,32768]{2,1,0:T(2,128)(2,1)} %reshape.315), calls=%async_computation.1 | async-start | bytes 1048576 | tf_op jit(solution)/shard_map/all_to_all | solution.py:149
  266.0 166.3 %copy-start.14 = (f32[1024]{0:T(1024)}, f32[1024]{0:T(1024)S(1)}, u32[]{:S(2)}) copy-start(f32[1024]{0:T(1024)S(1)} %convert_element_type.143) | copy-start | bytes 12292
  266.0 103.5 %copy-start.16 = (f32[1024]{0:T(1024)}, f32[1024]{0:T(1024)S(1)}, u32[]{:S(2)}) copy-start(f32[1024]{0:T(1024)S(1)} %convert_element_type.144) | copy-start | bytes 12292
  369.2 63.1 %copy-start.1 = (f32[256,1024]{1,0:T(8,128)}, f32[256,1024]{1,0:T(8,128)S(1)}, u32[]{:S(2)}) copy-start(f32[256,1024]{1,0:T(8,128)S(1)} %get-tuple-element.1066) | copy-start | bytes 3145732
  369.3 63.1 %copy-start.22 = (f32[256]{0:T(256)}, f32[256]{0:T(256)S(1)}, u32[]{:S(2)}) copy-start(f32[256]{0:T(256)S(1)} %broadcast_multiply_fusion.4) | copy-start | bytes 3076
  369.5 62.9 %copy-start.26 = (f32[256]{0:T(256)}, f32[256]{0:T(256)S(1)}, u32[]{:S(2)}) copy-start(f32[256]{0:T(256)S(1)} %add_rsqrt_fusion) | copy-start | bytes 3076
  369.6 47.7 %copy-start.11 = (bf16[256,1024]{1,0:T(8,128)(2,1)S(1)}, bf16[256,1024]{1,0:T(8,128)(2,1)}, u32[]{:S(2)}) copy-start(bf16[256,1024]{1,0:T(8,128)(2,1)} %param.25) | copy-start | bytes 1572868
  417.3 11.8 copy-start.37
  429.2 3.2 copy-start.13
  429.2 5.3 copy-start.9
  436.0 15.9 %all-to-all-start.2 = ((bf16[256,4,256]{2,0,1:T(8,128)(2,1)}), bf16[256,4,256]{2,0,1:T(8,128)(2,1)S(1)}, u32[]{:S(2)}, u32[]{:S(2)}) async-start(bf16[256,4,256]{2,0,1:T(8,128)(2,1)} %bitcast.133), calls=%async_computation.2 | async-start | bytes 1048576 | tf_op jit(solution)/shard_map/all_to_all | solution.py:205
  440.0 436.0 %reduce-scatter.6.cloned.1.call-start = ((), (), s32[]{:S(2)}) async-start(), calls=%async_computation.14 | async-start | bytes 9437184 | tf_op jit(solution)/shard_map/reduce_scatter | solution.py:257
  525.9 2.7 copy-start
  554.2 1.2 copy-start.4
  554.2 1.4 copy-start.10
  554.2 461.8 %reduce-scatter.10.cloned.1.call-start = ((), (), s32[]{:S(2)}) async-start(), calls=%async_computation.16 | async-start | bytes 4325376 | tf_op jit(solution)/shard_map/reduce_scatter | solution.py:303
  558.3 624.4 %reduce-scatter.8.cloned.1.call-start = ((), (), s32[]{:S(2)}) async-start(), calls=%async_computation.15 | async-start | bytes 12976128 | tf_op jit(solution)/shard_map/reduce_scatter | solution.py:300
  877.3 47.2 %copy-start.6 = (bf16[256,1024]{1,0:T(8,128)(2,1)S(1)}, bf16[256,1024]{1,0:T(8,128)(2,1)}, u32[]{:S(2)}) copy-start(bf16[256,1024]{1,0:T(8,128)(2,1)} %param.24) | copy-start | bytes 1572868
  877.3 47.2 %copy-start.19 = (f32[1024]{0:T(1024)S(1)}, f32[1024]{0:T(1024)}, u32[]{:S(2)}) copy-start(f32[1024]{0:T(1024)} %copy-done.18) | copy-start | bytes 12292
  877.3 47.2 %copy-start.21 = (f32[1024]{0:T(1024)S(1)}, f32[1024]{0:T(1024)}, u32[]{:S(2)}) copy-start(f32[1024]{0:T(1024)} %copy-done.20) | copy-start | bytes 12292
  877.3 47.2 %copy-start.25 = (f32[256]{0:T(256)S(1)}, f32[256]{0:T(256)}, u32[]{:S(2)}) copy-start(f32[256]{0:T(256)} %copy-done.24) | copy-start | bytes 3076
  877.4 47.2 %copy-start.29 = (f32[256]{0:T(256)S(1)}, f32[256]{0:T(256)}, u32[]{:S(2)}) copy-start(f32[256]{0:T(256)} %copy-done.28) | copy-start | bytes 3076
  923.4 1.2 copy-start.7
  931.1 1.0 copy-start.12
  931.1 438.9 %reduce-scatter.14.cloned.1.call-start = ((), (), s32[]{:S(2)}) async-start(), calls=%async_computation.18 | async-start | bytes 17301504 | tf_op jit(solution)/shard_map/reduce_scatter | solution.py:198
  942.9 1.2 copy-start.2
  942.9 1.2 copy-start.15
  942.9 1.2 copy-start.17
  942.9 1.2 copy-start.23
  942.9 1.2 copy-start.27
  943.0 614.3 %reduce-scatter.12.cloned.1.call-start = ((), (), s32[]{:S(2)}) async-start(), calls=%async_computation.17 | async-start | bytes 17301504 | tf_op jit(solution)/shard_map/reduce_scatter | solution.py:196
  954.7 8.4 copy-start.8
  963.4 5.1 copy-start.30
  963.4 5.1 copy-start.31
  963.4 5.1 copy-start.32
  963.4 5.1 copy-start.33
  963.4 5.1 copy-start.34
  (2 other events, 1.6 us)
Sparse Core Ops, SparseCore 0:
  10.9 69.8 all-gather.6
  135.6 53.8 all-gather.8
  192.3 55.6 all-gather.10
  250.7 83.0 all-gather.12
  336.6 80.6 all-gather.14
  554.4 321.5 reduce-scatter.5
  878.9 119.9 reduce-scatter.9
  1006.6 176.0 reduce-scatter.7
  1185.5 184.4 reduce-scatter.13
  1372.7 184.4 reduce-scatter.11
